TPU v7x, 32 devices: a whole 2x2x4 slice. The times are simulated.
32 devices in a mesh: groups: 2 (over y), node: 4 (over z), rep: 4 (over x, core).
Axes of the slice: x: 2, y: 2, z: 4, core: 2. Of those that a mesh axis runs over, the one named last changes fastest.
Arguments:
- node_states: bfloat16 [8, 512, 512], P(('groups', 'rep'), 'node'), parts along dimension 0, may hold values from -6 to 6
- cotangent: bfloat16 [8, 512, 512], P(('groups', 'rep'), 'node'), parts along dimension 0, may hold values from -1.1953125 to 1.1953125
- reach_blocks: int32 [8, 8, 8], P(('groups', 'rep'), 'node'), parts along dimension 0, may hold values from 0 to 7, as said below
- reach_count: int32 [8, 8], P(('groups', 'rep'), 'node'), parts along dimension 0, may hold values from 1 to 8, as said below
- level_start: int32 [8, 17], P(('groups', 'rep')), parts along dimension 0, may hold values from 0 to 512, as said below
- query_weight: bfloat16 [512, 256], replicated, may hold values from -0.25 to 0.25
- key_weight: bfloat16 [512, 256], replicated, may hold values from -0.25 to 0.25
- value_weight: bfloat16 [512, 256], replicated, may hold values from -0.25 to 0.25
- out_weight: bfloat16 [256, 512], replicated, may hold values from -0.375 to 0.375
- bias_table: float32 [4, 32], replicated, may hold values from -4 to 412
Outputs:
- updated: bfloat16 [8, 512, 512], P(('groups', 'rep'), 'node'), parts along dimension 0
- node_state_gradient: bfloat16 [8, 512, 512], P(('groups', 'rep'), 'node'), parts along dimension 0
- grad_query: float32 [1024, 256], P('groups'), parts along dimension 0
- grad_key: float32 [1024, 256], P('groups'), parts along dimension 0
- grad_value: float32 [1024, 256], P('groups'), parts along dimension 0
- grad_out: float32 [512, 512], P('groups'), parts along dimension 0
There are 2 independent parts, one for each index of `groups`. A program takes and returns all parts, laid end to end along the dimension named above; an argument that names none is the same for every part. Nothing has to cross between parts.
Inputs may be any that keep to these rules, and one draw needn't show every extreme that they name: `reach_blocks`: in row b of a graph, entry 0 is b, entries 1 to min(b, 7) are distinct blocks below b, and any later entries are b. `reach_count`: row b holds at most b + 1; row 7 of every graph holds 8. `level_start`: strictly increasing; entry 0 is 0 and entry 16 is 512.
All inputs are finite; a program needn't handle non-finite values.
Results may differ from a plain program's by a relative error of at most 0.011.
Values may be sent and summed in bfloat16 or wider, within the bound.
No kernel may reach another device: no remote copies, remote signals or barrier semaphores. Data moves between devices by JAX's collectives and lax.ppermute only.
A program may use at most 64 MiB of HBM per device.

v0:
```python
import jax
import jax.numpy as jnp
from jax import lax
from jax.sharding import PartitionSpec as P

HEADS = 4
HEAD = 64
BLOCK = 64
DIST = 32
EPS = 1e-05
NEG = -1e30
HIGH = lax.Precision.HIGHEST
CONTRACT_ROWS = (((0,), (0,)), ((), ()))
CONTRACT_COLS = (((1,), (1,)), ((), ()))


def rows_product(left, right):
    return lax.dot_general(left, right, CONTRACT_ROWS, preferred_element_type=jnp.float32)


def cols_product(left, right):
    return lax.dot_general(left, right, CONTRACT_COLS, preferred_element_type=jnp.float32)


def expand(listed):
    return jnp.repeat(jnp.repeat(listed, BLOCK, axis=0), BLOCK, axis=1)


def level_tables(starts, total, bias_table):
    level_count = starts.shape[0] - 1
    places = jnp.arange(total, dtype=jnp.int32)
    inner = starts[1:level_count]
    levels = jnp.sum((places[:, None] >= inner[None, :]).astype(jnp.int32), axis=1)
    marks = jnp.arange(level_count, dtype=jnp.int32)
    onehot = (levels[:, None] == marks[None, :]).astype(jnp.float32)
    spread = jnp.clip(marks[:, None] - marks[None, :], 0, DIST - 1)
    picks = (spread[:, :, None] == jnp.arange(DIST, dtype=jnp.int32)[None, None, :]).astype(
        jnp.float32
    )
    level_bias = jnp.einsum("hd,abd->hab", bias_table, picks, precision=HIGH)
    return (levels, onehot, level_bias)


def bias_block(row_onehot, head_bias, col_onehot):
    row_part = jnp.dot(row_onehot, head_bias, precision=HIGH)
    return lax.dot_general(row_part, col_onehot, CONTRACT_COLS, precision=HIGH)


def on_device(
    node_states,
    cotangent,
    reach_blocks,
    reach_count,
    level_start,
    query_weight,
    key_weight,
    value_weight,
    out_weight,
    bias_table,
):
    states = node_states[0]
    grads_in = cotangent[0]
    blocks = reach_blocks[0]
    counts = reach_count[0]
    starts = level_start[0]
    rows_dev = states.shape[0]
    width = query_weight.shape[1]
    total = rows_dev * lax.axis_size("node")
    offset = lax.axis_index("node") * rows_dev
    scale = HEAD ** (-0.5)
    key_blocks = total // BLOCK
    states_single_float = states.astype(jnp.float32)
    inverse_norm_scale = lax.rsqrt(
        jnp.mean(states_single_float * states_single_float, axis=1, keepdims=True) + EPS
    )
    centered_states = states_single_float * inverse_norm_scale
    normalized_states = centered_states.astype(jnp.bfloat16)
    queries = jnp.dot(normalized_states, query_weight, preferred_element_type=jnp.float32).astype(
        jnp.bfloat16
    )
    keys = jnp.dot(normalized_states, key_weight, preferred_element_type=jnp.float32).astype(
        jnp.bfloat16
    )
    values = jnp.dot(normalized_states, value_weight, preferred_element_type=jnp.float32).astype(
        jnp.bfloat16
    )
    keys_all, values_all = (
        lax.all_gather(keys, "node", axis=0, tiled=True),
        lax.all_gather(values, "node", axis=0, tiled=True),
    )
    levels, onehot, level_bias = level_tables(starts, total, bias_table)
    positions = jnp.arange(total, dtype=jnp.int32)
    local = jnp.arange(rows_dev, dtype=jnp.int32)
    row_ids = offset + local
    row_levels = lax.dynamic_slice_in_dim(levels, offset, rows_dev, 0)
    row_onehot = lax.dynamic_slice_in_dim(onehot, offset, rows_dev, 0)
    slots = jnp.arange(blocks.shape[1], dtype=jnp.int32)
    live = slots[None, :] < counts[:, None]
    kinds = jnp.arange(key_blocks, dtype=jnp.int32)
    listed = jnp.any((blocks[:, :, None] == kinds[None, None, :]) & live[:, :, None], axis=1)
    visible = expand(listed) & (
        (levels[None, :] < row_levels[:, None]) | (positions[None, :] == row_ids[:, None])
    )
    prob_list = []
    lse_list = []
    mixed_list = []
    for head in range(HEADS):
        lower = head * HEAD
        scores = (
            cols_product(queries[:, lower : lower + HEAD], keys_all[:, lower : lower + HEAD])
            * scale
        )
        scores = scores + bias_block(row_onehot, level_bias[head], onehot)
        scores = jnp.where(visible, scores, NEG)
        peak = jnp.max(scores, axis=1, keepdims=True)
        mass = jnp.sum(jnp.where(visible, jnp.exp(scores - peak), 0.0), axis=1, keepdims=True)
        lse = peak + jnp.log(mass)
        probs = jnp.where(visible, jnp.exp(scores - lse), 0.0).astype(jnp.bfloat16)
        prob_list.append(probs)
        lse_list.append(lse)
        mixed_list.append(
            jnp.dot(probs, values_all[:, lower : lower + HEAD], preferred_element_type=jnp.float32)
        )
    mixed = jnp.concatenate(mixed_list, axis=1).astype(jnp.bfloat16)
    updated = (
        states_single_float + jnp.dot(mixed, out_weight, preferred_element_type=jnp.float32)
    ).astype(jnp.bfloat16)
    partial_out = rows_product(mixed, grads_in)
    d_mixed = cols_product(grads_in, out_weight).astype(jnp.bfloat16)
    score_grads = []
    delta_list = []
    query_grads = []
    for head in range(HEADS):
        lower = head * HEAD
        mixed_head = d_mixed[:, lower : lower + HEAD]
        delta = jnp.sum(
            mixed_head.astype(jnp.float32) * mixed[:, lower : lower + HEAD].astype(jnp.float32),
            axis=1,
            keepdims=True,
        )
        d_probs = cols_product(mixed_head, values_all[:, lower : lower + HEAD])
        d_scores = (prob_list[head].astype(jnp.float32) * (d_probs - delta)).astype(jnp.bfloat16)
        score_grads.append(d_scores)
        delta_list.append(delta)
        query_grads.append(
            jnp.dot(d_scores, keys_all[:, lower : lower + HEAD], preferred_element_type=jnp.float32)
            * scale
        )
    d_queries = jnp.concatenate(query_grads, axis=1).astype(jnp.bfloat16)
    key_pieces = []
    value_pieces = []
    for head in range(HEADS):
        lower = head * HEAD
        score_part = score_grads[head]
        prob_part = prob_list[head]
        key_pieces.append(rows_product(score_part, queries[:, lower : lower + HEAD]) * scale)
        value_pieces.append(rows_product(prob_part, d_mixed[:, lower : lower + HEAD]))
    key_value_grads = lax.psum_scatter(
        jnp.concatenate(key_pieces + value_pieces, axis=1).astype(jnp.bfloat16),
        "node",
        scatter_dimension=0,
        tiled=True,
    ).astype(jnp.float32)
    d_keys = key_value_grads[:, :width].astype(jnp.bfloat16)
    d_values = key_value_grads[:, width:].astype(jnp.bfloat16)
    normalized_gradient = (
        cols_product(d_queries, query_weight)
        + cols_product(d_keys, key_weight)
        + cols_product(d_values, value_weight)
    )
    node_state_gradient = (
        grads_in.astype(jnp.float32)
        + inverse_norm_scale
        * (
            normalized_gradient
            - centered_states
            * jnp.mean(normalized_gradient * centered_states, axis=1, keepdims=True)
        )
    ).astype(jnp.bfloat16)
    partial_query = rows_product(normalized_states, d_queries)
    partial_key = rows_product(normalized_states, d_keys)
    partial_value = rows_product(normalized_states, d_values)
    total_query, total_key, total_value, total_out = lax.psum(
        (partial_query, partial_key, partial_value, partial_out), ("node", "rep")
    )
    return (
        updated[None],
        node_state_gradient[None],
        total_query,
        total_key,
        total_value,
        total_out,
    )


def solution(mesh):
    in_specs = (
        P(("groups", "rep"), "node", None),
        P(("groups", "rep"), "node", None),
        P(("groups", "rep"), "node", None),
        P(("groups", "rep"), "node"),
        P(("groups", "rep"), None),
        P(),
        P(),
        P(),
        P(),
        P(),
    )
    out_specs = (
        P(("groups", "rep"), "node", None),
        P(("groups", "rep"), "node", None),
        P("groups", None),
        P("groups", None),
        P("groups", None),
        P("groups", None),
    )
    return jax.shard_map(
        on_device, mesh=mesh, in_specs=in_specs, out_specs=out_specs, check_vma=False
    )
```

profile of v0, /device:TPU:0, one launch (start us, length us, event | category | flops | bytes accessed | tf_op | source)
XLA Modules:
  0.0 189.7 jit_solution(12456625626089858018)
XLA Ops:
  7.3 0.6 copy-done.12
  8.0 0.7 copy-done.10
  8.9 0.6 copy-done.13
  9.5 1.0 fusion.42
  11.0 0.6 copy-done.11
  11.6 0.6 convolution_bitcast_fusion
  13.4 0.3 convolution_convert_fusion.3
  13.6 0.3 copy-done.5
  14.1 0.2 convolution_convert_fusion.1
  14.4 15.6 %all_gather.7 = bf16[512,256]{1,0:T(8,128)(2,1)S(1)} all-gather(bf16[128,256]{1,0:T(8,128)(2,1)S(1)} %convolution_convert_fusion.1), channel_id=1, replica_groups=mesh['groups'=2,'node'=4,'rep'=4] {'node'}, dimensions={0}, use_global_device_ids=true | all-gather | bytes 327680 | tf_op jit(solution)/shard_map/all_gather | solution.py:89
  30.0 14.6 %all_gather.6 = bf16[512,256]{1,0:T(8,128)(2,1)S(1)} all-gather(bf16[128,256]{1,0:T(8,128)(2,1)S(1)} %convolution_convert_fusion.2), channel_id=1, replica_groups=mesh['groups'=2,'node'=4,'rep'=4] {'node'}, dimensions={0}, use_global_device_ids=true | all-gather | bytes 327680 | tf_op jit(solution)/shard_map/all_gather | solution.py:88
  44.6 0.4 fusion.46
  45.0 0.4 fusion.43
  45.4 0.3 fusion.124
  45.7 0.4 fusion.127
  46.0 0.4 fusion.44
  46.4 0.3 fusion.126
  46.7 0.4 fusion.45
  47.1 0.4 fusion.125
  47.5 0.4 select_reduce_fusion.3
  47.9 0.3 select_convert_fusion.3
  48.2 0.3 convolution_convert_fusion.10
  48.7 0.3 convolution_convert_fusion.8
  49.0 0.4 copy-done.3
  49.9 0.2 multiply_reduce_fusion.3
  50.3 0.3 fusion.14
  50.8 0.3 fusion.16
  51.3 0.3 fusion.21
  51.8 0.3 fusion.25
  52.7 1.0 copy.27
  54.0 0.3 fusion.31
  54.3 0.3 fusion.33
  54.8 0.2 fusion.105
  55.0 1.0 fusion.50
  56.0 1.1 fusion.104
  57.1 19.4 %reduce-scatter.4.cloned.1.call-done = bf16[128,512]{1,0:T(8,128)(2,1)} async-done(((bf16[512,512]{1,0:T(8,128)(2,1)}), bf16[128,512]{1,0:T(8,128)(2,1)}) %reduce-scatter.4.cloned.1.call-update) | async-done | bytes 131088
  76.5 2.0 %fusion.78 = f32[512,256]{1,0:T(8,128)} fusion(bf16[128,512]{1,0:T(8,128)(2,1)} %reduce-scatter.4.cloned.1.call-done, bf16[1,128,512]{2,1,0:T(8,128)(2,1)S(1)} %copy-done.1, f32[128]{0:T(128)S(1)} %add_rsqrt_fusion), kind=kOutput, calls=%fused_computation.125 | convolution fusion | flops 33751040 | bytes 721408 | tf_op jit(solution)/shard_map/dot_general | solution.py:18
  78.5 1.1 fusion.75
  79.6 0.9 fusion.17
  80.7 0.3 fusion.37
  81.1 0.8 fusion.49
  81.9 95.8 %all-reduce.3.cloned.1.call-done = (f32[512,256]{1,0:T(8,128)}, f32[512,256]{1,0:T(8,128)}, f32[512,256]{1,0:T(8,128)}, f32[256,512]{1,0:T(8,128)}) async-done(((f32[512,256]{1,0:T(8,128)}, f32[512,256]{1,0:T(8,128)}, f32[512,256]{1,0:T(8,128)}, f32[256,512]{1,0:T(8,128)}), (f32[512,256]{1,0:T(8,128)}, f32[512,256]{1,0:T(8,128)}, f32[512,256]{1,0:T(8,128)}, ...) | async-done | bytes 2097168 | tf_op jit(solution)/shard_map/psum | solution.py:183
  177.7 1.9 %copy.53 = f32[512,256]{1,0:T(8,128)} copy(f32[512,256]{1,0:T(8,128)} %get-tuple-element.43) | data formatting | bytes 1048576
  179.6 0.8 copy.54
  180.4 0.4 copy-done.7
  180.8 0.8 copy.55
  181.6 0.4 copy-done.6
  182.0 0.8 copy.56
  (60 shorter events, 5.0 us)
Async XLA Ops:
  7.2 7.0 %copy-start = (bf16[512,256]{1,0:T(8,128)(2,1)S(1)}, bf16[512,256]{1,0:T(8,128)(2,1)}, u32[]{:S(2)}) copy-start(bf16[512,256]{1,0:T(8,128)(2,1)} %param.17) | copy-start | bytes 786436
  7.2 69.3 %reduce-scatter.4.cloned.1.call-start = ((), (), s32[]{:S(2)}) async-start(), calls=%async_computation.1 | async-start | bytes 655360
  7.3 0.7 copy-start.12
  8.0 0.7 copy-start.10
  8.8 0.7 copy-start.13
  10.9 0.7 copy-start.11
  11.6 1.7 copy-start.4
  12.3 1.0 copy-start.1
  12.9 1.0 copy-start.5
  48.5 1.0 copy-start.3
  48.7 0.9 copy-start.2
  53.7 123.9 %all-reduce.3.cloned.1.call-start = ((), (), s32[]{:S(2)}) async-start(), calls=%async_computation.2 | async-start | bytes 4194304 | tf_op jit(solution)/shard_map/psum | solution.py:183
  76.5 2.0 %copy-start.9 = (bf16[128,512]{1,0:T(8,128)(2,1)S(1)}, bf16[128,512]{1,0:T(8,128)(2,1)}, u32[]{:S(2)}) copy-start(bf16[128,512]{1,0:T(8,128)(2,1)} %reduce-scatter.4.cloned.1.call-done) | copy-start | bytes 393220
  177.6 1.9 %copy-start.8 = (f32[512,256]{1,0:T(8,128)S(1)}, f32[512,256]{1,0:T(8,128)}, u32[]{:S(2)}) copy-start(f32[512,256]{1,0:T(8,128)} %get-tuple-element.44) | copy-start | bytes 1572868
  179.6 1.2 copy-start.7
  180.8 1.2 copy-start.6
Sparse Core Ops, SparseCore 0:
  53.8 22.5 reduce-scatter.3
  81.0 96.5 all-reduce.2
where the time goes:
time: 190 us
  waiting for transfers between devices  115 us (61%)
  blocking collectives  30.2 us (16%)
  matrix products  16.7 us (9%)
  between operations  14.3 us (8%)
  local copies, waits for them, and re-layouts  10.3 us (5%)
  other arithmetic  2.95 us (2%)
    psum x1, waiting for transfers between devices, on_device(): lax.psum((partial_query, partial_key, partial_value, partial_out), ('node...  95.8 us
    unnamed x3, waiting for transfers between devices  19.4 us
    all_gather x1, blocking collectives, on_device(): lax.all_gather(values, 'node', axis=0, tiled=True)  15.6 us
    all_gather x1, blocking collectives, on_device(): lax.all_gather(keys, 'node', axis=0, tiled=True)  14.6 us
    unnamed x33, local copies, waits for them, and re-layouts  9.64 us
    dot_general x12, matrix products, rows_product(): lax.dot_general(left, right, CONTRACT_ROWS, preferred_element_type=jnp.fl...  6.81 us
  transfers between devices with their start and end apart: 2, of which 2 were waited for; matrix products, arithmetic and copies ran while one was open for 3% of the time, Pallas kernels for 0%

commit v1 on v0

--- a/solution.py
+++ b/solution.py
@@ -84,8 +84,43 @@
     values = jnp.dot(normalized_states, value_weight, preferred_element_type=jnp.float32).astype(
         jnp.bfloat16
     )
+
+    def note_loops(lane_axis, field):
+        m_next, item_now, current_block = (
+            lax.axis_size(lane_axis),
+            lax.axis_index(lane_axis),
+            field.shape[0],
+        )
+        n_now = top = field
+        tick = 1
+        big = lax.dynamic_update_slice_in_dim(
+            jnp.zeros(
+                [dev_j * m_next if j == 0 else dev_j for j, dev_j in enumerate(field.shape)],
+                field.dtype,
+            ),
+            field,
+            item_now * current_block,
+            axis=0,
+        )
+        while tick < m_next // 2 + 1:
+            n_now = lax.ppermute(
+                n_now, lane_axis, perm=[(j, (j + 1) % m_next) for j in range(m_next)]
+            )
+            big = lax.dynamic_update_slice_in_dim(
+                big, n_now, (item_now - tick) % m_next * current_block, axis=0
+            )
+            if 2 * tick < m_next:
+                top = lax.ppermute(
+                    top, lane_axis, perm=[(j, (j - 1) % m_next) for j in range(m_next)]
+                )
+                big = lax.dynamic_update_slice_in_dim(
+                    big, top, (item_now + tick) % m_next * current_block, axis=0
+                )
+            tick += 1
+        return big
+
     keys_all, values_all = (
-        lax.all_gather(keys, "node", axis=0, tiled=True),
+        note_loops("node", keys),
         lax.all_gather(values, "node", axis=0, tiled=True),
     )
     levels, onehot, level_bias = level_tables(starts, total, bias_table)

time: 190 us -> 182 us (0.958)
  blocking collectives: 30.2 us -> 14.3 us
  starting transfers between devices: 0.08 us -> 5.27 us
  waiting for transfers between devices: 115 us -> 119 us
    all_gather x1 -> x0, blocking collectives: 14.6 us -> none  [on_device(): lax.all_gather(keys, 'node', axis=0, tiled=True)]
    ppermute x0 -> x3, waiting for transfers between devices: none -> 6.01 us  [the longest x2 6.01 us: note_loops(): lax.ppermute(n_now, lane_axis, perm=[(j, (j + 1) % m_next) for j in range...]
    ppermute x0 -> x3, starting transfers between devices: none -> 5.19 us  [the longest x2 3.1 us: note_loops(): lax.ppermute(n_now, lane_axis, perm=[(j, (j + 1) % m_next) for j in range...]
    unnamed x3, waiting for transfers between devices: 19.4 us -> 17.3 us
  transfers between devices with their start and end apart: 2 -> 5, of which waited for: 2 -> 3; matrix products, arithmetic and copies ran while one was open for 3% -> 5% of each run, Pallas kernels for 0% -> 0%
where the time goes in v1:
time: 182 us
  waiting for transfers between devices  119 us (65%)
  matrix products  16.7 us (9%)
  between operations  14.4 us (8%)
  blocking collectives  14.3 us (8%)
  local copies, waits for them, and re-layouts  8.85 us (5%)
  starting transfers between devices  5.27 us (3%)
  other arithmetic  2.99 us (2%)
    psum x1, waiting for transfers between devices, on_device(): lax.psum((partial_query, partial_key, partial_value, partial_out), ('node...  95.7 us
    unnamed x3, waiting for transfers between devices  17.3 us
    all_gather x1, blocking collectives, on_device(): lax.all_gather(values, 'node', axis=0, tiled=True)  14.3 us
    unnamed x33, local copies, waits for them, and re-layouts  8.18 us
    dot_general x12, matrix products, rows_product(): lax.dot_general(left, right, CONTRACT_ROWS, preferred_element_type=jnp.fl...  6.83 us
    ppermute x2, waiting for transfers between devices, note_loops(): lax.ppermute(n_now, lane_axis, perm=[(j, (j + 1) % m_next) for j in range...  6.01 us
  transfers between devices with their start and end apart: 5, of which 3 were waited for; matrix products, arithmetic and copies ran while one was open for 5% of the time, Pallas kernels for 0%

profile of v1, /device:TPU:0, one launch (start us, length us, event | category | flops | bytes accessed | tf_op | source)
XLA Modules:
  0.0 181.6 jit_solution(5783134919929283896)
XLA Ops:
  7.2 1.0 fusion.42
  8.3 0.9 copy-done.1
  9.2 0.2 constant_dynamic-update-slice_fusion.3
  9.4 3.1 %collective-permute-start = (bf16[128,256]{1,0:T(8,128)(2,1)S(1)}, bf16[128,256]{1,0:T(8,128)(2,1)S(1)}, u32[]{:S(2)}, u32[]{:S(2)}) collective-permute-start(bf16[128,256]{1,0:T(8,128)(2,1)S(1)} %get-tuple-element.27), channel_id=1, source_target_pairs={{0,4},{4,8},{8,12},{12,0},{1,5},{5,9},{9,13},{13,1},{2,6},{6,10},{... | collective-permute-start | bytes 196616 | tf_op jit(solution)/shard_map/ppermute | solution.py:106
  12.5 2.1 %collective-permute-start.1 = (bf16[128,256]{1,0:T(8,128)(2,1)S(1)}, bf16[128,256]{1,0:T(8,128)(2,1)S(1)}, u32[]{:S(2)}, u32[]{:S(2)}) collective-permute-start(bf16[128,256]{1,0:T(8,128)(2,1)S(1)} %get-tuple-element.27), channel_id=1, source_target_pairs={{0,12},{4,0},{8,4},{12,8},{1,13},{5,1},{9,5},{13,9},{2,14},{6,2},{... | collective-permute-start | bytes 196616 | tf_op jit(solution)/shard_map/ppermute | solution.py:113
  14.7 0.6 copy-done.12
  16.1 0.6 convolution_bitcast_fusion
  17.0 0.2 convolution_convert_fusion.3
  17.4 0.2 fusion.90
  18.1 0.3 convolution_convert_fusion.1
  18.4 0.4 fusion.46
  18.8 0.4 fusion.43
  19.2 0.4 fusion.44
  19.6 0.4 fusion.45
  20.1 0.4 copy-done.2
  20.7 14.3 %all_gather.3 = bf16[512,256]{1,0:T(8,128)(2,1)S(1)} all-gather(bf16[128,256]{1,0:T(8,128)(2,1)S(1)} %convolution_convert_fusion.1), channel_id=1, replica_groups=mesh['groups'=2,'node'=4,'rep'=4] {'node'}, dimensions={0}, use_global_device_ids=true | all-gather | bytes 327680 | tf_op jit(solution)/shard_map/all_gather | solution.py:124
  35.1 6.0 %collective-permute-done.2 = bf16[128,256]{1,0:T(8,128)(2,1)S(1)} collective-permute-done((bf16[128,256]{1,0:T(8,128)(2,1)S(1)}, bf16[128,256]{1,0:T(8,128)(2,1)S(1)}, u32[]{:S(2)}, u32[]{:S(2)}) %collective-permute-start.2) | collective-permute-done | bytes 65568 | tf_op jit(solution)/shard_map/ppermute | solution.py:106
  41.1 0.4 fusion.127
  41.5 0.3 fusion.126
  41.7 0.4 fusion.125
  42.1 0.3 fusion.124
  42.4 0.4 select_reduce_fusion.3
  42.8 0.3 select_convert_fusion.3
  43.1 0.3 convolution_convert_fusion.10
  43.6 0.3 convolution_convert_fusion.8
  44.8 0.3 fusion.14
  45.1 0.3 fusion.31
  45.6 0.3 fusion.16
  45.8 0.3 fusion.21
  46.3 0.3 fusion.25
  47.2 1.0 copy.27
  48.3 0.3 fusion.33
  48.8 0.2 fusion.105
  49.0 1.0 fusion.50
  50.0 1.1 fusion.104
  51.2 17.3 %reduce-scatter.4.cloned.1.call-done = bf16[128,512]{1,0:T(8,128)(2,1)} async-done(((bf16[512,512]{1,0:T(8,128)(2,1)}), bf16[128,512]{1,0:T(8,128)(2,1)}) %reduce-scatter.4.cloned.1.call-update) | async-done | bytes 131088
  68.5 2.0 %fusion.78 = f32[512,256]{1,0:T(8,128)} fusion(bf16[128,512]{1,0:T(8,128)(2,1)} %reduce-scatter.4.cloned.1.call-done, bf16[1,128,512]{2,1,0:T(8,128)(2,1)S(1)} %copy-done.1, f32[128]{0:T(128)S(1)} %add_rsqrt_fusion), kind=kOutput, calls=%fused_computation.125 | convolution fusion | flops 33751040 | bytes 721408 | tf_op jit(solution)/shard_map/dot_general | solution.py:18
  70.5 1.1 fusion.75
  71.6 0.9 fusion.17
  72.7 0.3 fusion.37
  73.1 0.8 fusion.49
  73.9 95.7 %all-reduce.3.cloned.1.call-done = (f32[512,256]{1,0:T(8,128)}, f32[512,256]{1,0:T(8,128)}, f32[512,256]{1,0:T(8,128)}, f32[256,512]{1,0:T(8,128)}) async-done(((f32[512,256]{1,0:T(8,128)}, f32[512,256]{1,0:T(8,128)}, f32[512,256]{1,0:T(8,128)}, f32[256,512]{1,0:T(8,128)}), (f32[512,256]{1,0:T(8,128)}, f32[512,256]{1,0:T(8,128)}, f32[512,256]{1,0:T(8,128)}, ...) | async-done | bytes 2097168 | tf_op jit(solution)/shard_map/psum | solution.py:218
  169.5 1.9 %copy.57 = f32[512,256]{1,0:T(8,128)} copy(f32[512,256]{1,0:T(8,128)} %get-tuple-element.45) | data formatting | bytes 1048576
  171.5 0.8 copy.58
  172.3 0.4 copy-done.7
  172.7 0.8 copy.59
  173.5 0.4 copy-done.6
  173.9 0.8 copy.60
  (69 shorter events, 4.8 us)
Async XLA Ops:
  7.2 1.2 copy-start
  7.2 61.3 %reduce-scatter.4.cloned.1.call-start = ((), (), s32[]{:S(2)}) async-start(), calls=%async_computation.1 | async-start | bytes 655360
  8.3 0.9 copy-start.1
  9.4 25.6 %collective-permute-start = (bf16[128,256]{1,0:T(8,128)(2,1)S(1)}, bf16[128,256]{1,0:T(8,128)(2,1)S(1)}, u32[]{:S(2)}, u32[]{:S(2)}) collective-permute-start(bf16[128,256]{1,0:T(8,128)(2,1)S(1)} %get-tuple-element.27), channel_id=1, source_target_pairs={{0,4},{4,8},{8,12},{12,0},{1,5},{5,9},{9,13},{13,1},{2,6},{6,10},{... | collective-permute-start | bytes 196616 | tf_op jit(solution)/shard_map/ppermute | solution.py:106
  12.5 22.5 %collective-permute-start.1 = (bf16[128,256]{1,0:T(8,128)(2,1)S(1)}, bf16[128,256]{1,0:T(8,128)(2,1)S(1)}, u32[]{:S(2)}, u32[]{:S(2)}) collective-permute-start(bf16[128,256]{1,0:T(8,128)(2,1)S(1)} %get-tuple-element.27), channel_id=1, source_target_pairs={{0,12},{4,0},{8,4},{12,8},{1,13},{5,1},{9,5},{13,9},{2,14},{6,2},{... | collective-permute-start | bytes 196616 | tf_op jit(solution)/shard_map/ppermute | solution.py:113
  14.6 0.7 copy-start.12
  14.6 1.0 copy-start.13
  14.6 1.1 copy-start.10
  14.6 1.5 copy-start.11
  14.6 2.3 %copy-start.5 = (bf16[512,256]{1,0:T(8,128)(2,1)S(1)}, bf16[512,256]{1,0:T(8,128)(2,1)}, u32[]{:S(2)}) copy-start(bf16[512,256]{1,0:T(8,128)(2,1)} %param.15) | copy-start | bytes 786436
  17.0 1.1 copy-start.3
  19.2 1.0 copy-start.4
  19.6 0.9 copy-start.2
  35.0 6.1 %collective-permute-start.2 = (bf16[128,256]{1,0:T(8,128)(2,1)S(1)}, bf16[128,256]{1,0:T(8,128)(2,1)S(1)}, u32[]{:S(2)}, u32[]{:S(2)}) collective-permute-start(bf16[128,256]{1,0:T(8,128)(2,1)S(1)} %collective-permute-done), channel_id=1, source_target_pairs={{0,4},{4,8},{8,12},{12,0},{1,5},{5,9},{9,13},{13,1},{2,6},{6,10},{... | collective-permute-start | bytes 196616 | tf_op jit(solution)/shard_map/ppermute | solution.py:106
  48.3 121.3 %all-reduce.3.cloned.1.call-start = ((), (), s32[]{:S(2)}) async-start(), calls=%async_computation.2 | async-start | bytes 4194304 | tf_op jit(solution)/shard_map/psum | solution.py:218
  68.5 2.0 %copy-start.9 = (bf16[128,512]{1,0:T(8,128)(2,1)S(1)}, bf16[128,512]{1,0:T(8,128)(2,1)}, u32[]{:S(2)}) copy-start(bf16[128,512]{1,0:T(8,128)(2,1)} %reduce-scatter.4.cloned.1.call-done) | copy-start | bytes 393220
  169.5 1.9 %copy-start.8 = (f32[512,256]{1,0:T(8,128)S(1)}, f32[512,256]{1,0:T(8,128)}, u32[]{:S(2)}) copy-start(f32[512,256]{1,0:T(8,128)} %get-tuple-element.46) | copy-start | bytes 1572868
  171.5 1.2 copy-start.7
  172.7 1.2 copy-start.6
Sparse Core Ops, SparseCore 0:
  48.4 20.0 reduce-scatter.3
  73.0 96.4 all-reduce.2
